TPU v7x, 32 devices: a whole 2x2x4 slice. The times are simulated.
32 devices in a mesh: slab: 8 (over z, y), subj: 2 (over core), tm: 2 (over x).
Axes of the slice: x: 2, y: 2, z: 4, core: 2. Of those that a mesh axis runs over, the one named last changes fastest.
Arguments:
- subject_data: bfloat16 [2, 16, 128, 2048], P('subj', 'slab', None, 'tm'), may hold values from -8 to 8
- template: bfloat16 [16, 128, 2048], P('slab', None, 'tm'), may hold values from -8 to 8
- neighbours: int32 [16, 27], P('slab'), may hold values from 0 to 15, as said below
- valid: int32 [16, 27], P('slab'), may hold values from 0 to 1, as said below
Outputs:
- new_template: bfloat16 [16, 128, 2048], P('slab', None, 'tm')
Inputs may be any that keep to these rules, and one draw needn't show every extreme that they name: `neighbours`: slots 9 l to 9 l + 8 of block b name blocks of the slab of b shifted by l - 1 (slabs hold 2 consecutive blocks); where that slab doesn't exist they name b itself. Slot 13 names b itself. `valid`: slot 13 is always 1; slots whose slab doesn't exist are 0.
All inputs are finite; a program needn't handle non-finite values.
Results may differ from a plain program's by a relative error of at most 0.007.
Values may be sent and summed in bfloat16 or wider, within the bound.
No kernel may reach another device: no remote copies, remote signals or barrier semaphores. Data moves between devices by JAX's collectives and lax.ppermute only.
A program may use at most 64 MiB of HBM per device.

v0:
```python
import jax
import jax.numpy as jnp
from jax import lax
from jax.sharding import PartitionSpec as P

ITERS = 3


def with_halo(cells, sides, width):
    for axis, dim in sides:
        count = lax.axis_size(axis)
        ends = count - 1
        head = lax.slice_in_dim(cells, 0, width, axis=dim)
        tail = lax.slice_in_dim(cells, cells.shape[dim] - width, cells.shape[dim], axis=dim)
        cells = jnp.concatenate(
            [
                lax.ppermute(tail, axis, [(i, (i + 1) % count) for i in range(ends)]),
                cells,
                lax.ppermute(head, axis, [((i + 1) % count, i) for i in range(ends)]),
            ],
            axis=dim,
        )
    return cells


def balance(cross, row_norm, col_norm, mask):
    width = cross.shape[-1]
    logits = cross * row_norm[None, :, None, None] * col_norm[:, None, :, :] / 0.03
    masked = mask[None, None, :, None]
    kernel = jnp.exp(logits) * masked
    target = masked / (width * jnp.sum(mask))
    filler = 1.0 - masked
    col_weight = jnp.ones((cross.shape[0], 1, cross.shape[2], width), jnp.float32)
    for step in range(ITERS):
        row_weight = 1.0 / width / jnp.sum(kernel * col_weight, axis=(2, 3), keepdims=True)
        col_weight = target / (jnp.sum(kernel * row_weight, axis=1, keepdims=True) + filler)
    flow = kernel * col_weight
    return (flow / jnp.sum(flow, axis=(2, 3), keepdims=True)).astype(jnp.bfloat16)


def square_sum(values):
    return jnp.einsum("...t,...t->...", values, values, preferred_element_type=jnp.float32)


def slot_cross(tmpl_block, extended, slots):
    whole = jnp.einsum("it,sejt->siej", tmpl_block, extended, preferred_element_type=jnp.float32)
    return jnp.take(whole, slots, axis=2)


def project(plan, extended, slots):
    places = (slots[:, None] == jnp.arange(extended.shape[1], dtype=jnp.int32)[None, :]).astype(
        jnp.float32
    )
    folded = jnp.einsum(
        "sikj,ke->siej", plan.astype(jnp.float32), places, precision=lax.Precision.HIGHEST
    )
    upper = folded.astype(jnp.bfloat16)
    lower = (folded - upper.astype(jnp.float32)).astype(jnp.bfloat16)
    total = jnp.einsum("siej,sejt->it", upper, extended, preferred_element_type=jnp.float32)
    return total + jnp.einsum("siej,sejt->it", lower, extended, preferred_element_type=jnp.float32)


def subject_mean(moved, count):
    total = lax.psum(moved, "subj")
    return (total / count).astype(jnp.bfloat16)


def on_device(subject_data, template, neighbours, valid):
    blocks_here = template.shape[0]
    share = blocks_here // lax.axis_size("tm")
    subjects_all = subject_data.shape[0] * lax.axis_size("subj")
    offsets = neighbours - (lax.axis_index("slab") - 1) * blocks_here
    mask_all = valid.astype(jnp.float32)
    first = lax.axis_index("tm") * share
    my_offsets = lax.dynamic_slice_in_dim(offsets, first, share, 0)
    my_mask = lax.dynamic_slice_in_dim(mask_all, first, share, 0)
    full_time = lax.all_gather(subject_data, "tm", axis=3, tiled=True)
    extended = with_halo(full_time, (("slab", 1),), blocks_here)
    mine = lax.all_to_all(template, "tm", split_axis=0, concat_axis=2, tiled=True)
    col_norm = lax.rsqrt(square_sum(extended) + 1e-06)
    row_norm = lax.rsqrt(square_sum(mine) + 1e-06)

    def one_block(inputs):
        tmpl_block, scale_rows, slots, mask = inputs
        cross = slot_cross(tmpl_block, extended, slots)
        plan = balance(cross, scale_rows, jnp.take(col_norm, slots, axis=1), mask)
        return project(plan, extended, slots)

    moved = lax.map(one_block, (mine, row_norm, my_offsets, my_mask))
    averaged = subject_mean(moved, subjects_all)
    return lax.all_to_all(averaged, "tm", split_axis=2, concat_axis=0, tiled=True)


def solution(mesh):
    placed = (
        P("subj", "slab", None, "tm"),
        P("slab", None, "tm"),
        P("slab", None),
        P("slab", None),
    )
    return jax.shard_map(
        on_device, mesh=mesh, in_specs=placed, out_specs=P("slab", None, "tm"), check_vma=False
    )
```

profile of v0, /device:TPU:0, one launch (start us, length us, event | category | flops | bytes accessed | tf_op | source)
XLA Modules:
  0.0 159.5 jit_solution(255287246146315666)
XLA Ops:
  6.5 0.7 all-gather.2.cloned.1.call-update
  7.3 4.2 %all-to-all-start = ((bf16[2,128,1024]{2,1,0:T(8,128)(2,1)}), bf16[2,128,1024]{2,1,0:T(8,128)(2,1)S(1)}, u32[]{:S(2)}, u32[]{:S(2)}) async-start(bf16[2,128,1024]{2,1,0:T(8,128)(2,1)} %param.5), calls=%async_computation | async-start | bytes 1048576 | tf_op jit(solution)/shard_map/all_to_all | solution.py:79
  11.5 21.4 %all-gather.2.cloned.1.call-done = bf16[1,2,128,2048]{3,2,1,0:T(8,128)(2,1)} async-done(((bf16[1,2,128,1024]{3,2,1,0:T(8,128)(2,1)}), bf16[1,2,128,2048]{3,2,1,0:T(8,128)(2,1)}) %all-gather.2.cloned.1.call-update) | async-done | bytes 1048592 | tf_op jit(solution)/shard_map/all_gather | solution.py:77
  32.9 1.3 collective-permute-start.1
  34.2 5.5 %collective-permute-start = (bf16[1,2,128,2048]{3,2,1,0:T(8,128)(2,1)}, bf16[1,2,128,2048]{3,2,1,0:T(8,128)(2,1)}, u32[]{:S(2)}, u32[]{:S(2)}) collective-permute-start(bf16[1,2,128,2048]{3,2,1,0:T(8,128)(2,1)} %all-gather.2.cloned.1.call-done), channel_id=1, source_target_pairs={{0,4},{4,8},{8,12},{12,16},{16,20},{20,24},{24,28},{1,5},{5,9},{9,... | collective-permute-start | bytes 3145736 | tf_op jit(solution)/shard_map/ppermute | solution.py:17
  39.7 0.7 broadcast_subtract_fusion
  40.4 0.7 convert_element_type.29
  41.1 0.6 fusion.25
  43.0 1.2 reshape.327
  44.5 15.2 %collective-permute-done.1 = bf16[1,2,128,2048]{3,2,1,0:T(8,128)(2,1)S(1)} collective-permute-done((bf16[1,2,128,2048]{3,2,1,0:T(8,128)(2,1)}, bf16[1,2,128,2048]{3,2,1,0:T(8,128)(2,1)S(1)}, u32[]{:S(2)}, u32[]{:S(2)}) %collective-permute-start.1) | collective-permute-done | bytes 1048608 | tf_op jit(solution)/shard_map/ppermute | solution.py:19
  59.7 22.5 %collective-permute-done = bf16[1,2,128,2048]{3,2,1,0:T(8,128)(2,1)} collective-permute-done((bf16[1,2,128,2048]{3,2,1,0:T(8,128)(2,1)}, bf16[1,2,128,2048]{3,2,1,0:T(8,128)(2,1)}, u32[]{:S(2)}, u32[]{:S(2)}) %collective-permute-start) | collective-permute-done | bytes 1048608 | tf_op jit(solution)/shard_map/ppermute | solution.py:17
  82.2 1.8 %fusion = f32[6,128]{1,0:T(8,128)S(1)} fusion(bf16[1,2,128,2048]{3,2,1,0:T(8,128)(2,1)S(1)} %collective-permute-done.1, bf16[1,2,128,2048]{3,2,1,0:T(8,128)(2,1)S(1)} %copy-done, bf16[1,2,128,2048]{3,2,1,0:T(8,128)(2,1)} %collective-permute-done), kind=kLoop, calls=%fused_computation.3 | loop fusion | flops 7863552 | bytes 3148800 | tf_op jit(solution)/shard_map/...t,...t->.../dot_general | solution.py:42
  84.0 0.6 gather_fusion.1
  84.6 2.3 %convolution_bitcast_fusion.3 = f32[128,6,128]{0,2,1:T(8,128)S(1)} fusion(bf16[128,2048,1]{1,0,2:T(8,128)(2,1)} %reshape.327, bf16[1,2,128,2048]{3,2,1,0:T(8,128)(2,1)S(1)} %collective-permute-done.1, bf16[1,2,128,2048]{3,2,1,0:T(8,128)(2,1)S(1)} %copy-done, bf16[1,2,128,2048]{3,2,1,0:T(8,128)(2,1)} %collective-permute-done), kind=kOutput, calls=%fused_computation.31 | convolution fusion | flops 405798912 | bytes 4063232 | tf_op jit(solution)/shard_map/while/body/eval_jaxpr/it,sejt->siej/dot_general | solution.py:46
  86.9 0.7 gather_fusion
  87.7 0.8 fusion.27
  88.5 1.4 multiply_reduce_fusion.5
  90.0 1.3 multiply_reduce_fusion.4
  91.3 1.4 multiply_reduce_fusion.3
  92.8 1.3 multiply_reduce_fusion.2
  94.1 1.4 multiply_reduce_fusion.1
  95.6 1.3 multiply_reduce_fusion
  96.9 1.3 fusion.15
  98.3 1.3 copy.17
  99.9 2.8 %convolution_bitcast_fusion = f32[128,2048]{1,0:T(8,128)S(1)} fusion(bf16[128,6,128]{2,1,0:T(8,128)(2,1)S(1)} %get-tuple-element.32, bf16[1,2,128,2048]{3,2,1,0:T(8,128)(2,1)} %copy-done.2, bf16[1,2,128,2048]{3,2,1,0:T(8,128)(2,1)} %all-gather.2.cloned.1.call-done, bf16[1,2,128,2048]{3,2,1,0:T(8,128)(2,1)} %collective-permute-done), kind=kOutput, calls=%fused_computation.5 | convolution fusion | flops 405798912 | bytes 4390912 | tf_op jit(solution)/shard_map/while/body/eval_jaxpr/siej,sejt->it/dot_general | solution.py:60
  102.7 3.0 %fusion.2 = f32[1,128,2048]{2,1,0:T(8,128)} fusion(f32[128,2048]{1,0:T(8,128)S(1)} %convolution_bitcast_fusion, bf16[128,6,128]{2,1,0:T(8,128)(2,1)S(1)} %get-tuple-element.23, bf16[1,2,128,2048]{3,2,1,0:T(8,128)(2,1)S(1)} %copy-done.3, bf16[1,2,128,2048]{3,2,1,0:T(8,128)(2,1)S(1)} %copy-done.1, bf16[1,2,128,2048]{3,2,1,0:T(8,128)(2,1)} %collective-permute-done), kind=kOutput, calls=%fused_computation.8 | convolution fusion | flops 406061056 | bytes 5439488 | tf_op jit(solution)/shard_map/while/body/eval_jaxpr/siej,sejt->it/dot_general | solution.py:59
  105.7 19.7 %all-reduce.2.cloned.1.call-done = f32[1,128,2048]{2,1,0:T(8,128)} async-done(((f32[1,128,2048]{2,1,0:T(8,128)}), f32[1,128,2048]{2,1,0:T(8,128)}) %all-reduce.2.cloned.1.call-update) | async-done | bytes 1048592 | tf_op jit(solution)/shard_map/psum | solution.py:64
  125.4 1.3 multiply_convert_fusion
  126.7 0.8 copy.20
  128.0 11.7 %reduce.12 = bf16[2048,128]{1,0:T(8,128)(2,1)S(1)} reduce(bf16[2048,1,128]{2,1,0:T(2,128)(2,1)S(1)} %bitcast.110, bf16[]{:T(256)} %broadcast.450), dimensions={1}, to_apply=%bitcast.98.reduce_sub_computation | reduce | bytes 1048578
  139.9 11.2 %all_to_all.33 = bf16[2,2,65536]{2,1,0:T(2,128)(2,1)S(1)} all-to-all(bf16[2,2,65536]{2,1,0:T(2,128)(2,1)S(1)} %reshape.335), channel_id=1, replica_groups=mesh['slab'=8,'subj'=2,'tm'=2] {'tm'}, dimensions={0} | all-to-all | bytes 1048576 | tf_op jit(solution)/shard_map/all_to_all | solution.py:91
  151.7 1.0 copy.21
  (34 shorter events, 2.8 us)
Async XLA Ops:
  6.5 26.4 %all-gather.2.cloned.1.call-start = ((), (), s32[]{:S(2)}) async-start(), calls=%async_computation.2 | async-start | bytes 1572864 | tf_op jit(solution)/shard_map/all_gather | solution.py:77
  7.3 35.2 %all-to-all-start = ((bf16[2,128,1024]{2,1,0:T(8,128)(2,1)}), bf16[2,128,1024]{2,1,0:T(8,128)(2,1)S(1)}, u32[]{:S(2)}, u32[]{:S(2)}) async-start(bf16[2,128,1024]{2,1,0:T(8,128)(2,1)} %param.5), calls=%async_computation | async-start | bytes 1048576 | tf_op jit(solution)/shard_map/all_to_all | solution.py:79
  11.5 113.9 %all-reduce.2.cloned.1.call-start = ((), (), s32[]{:S(2)}) async-start(), calls=%async_computation.3 | async-start | bytes 2097152 | tf_op jit(solution)/shard_map/psum | solution.py:64
  32.9 26.8 %collective-permute-start.1 = (bf16[1,2,128,2048]{3,2,1,0:T(8,128)(2,1)}, bf16[1,2,128,2048]{3,2,1,0:T(8,128)(2,1)S(1)}, u32[]{:S(2)}, u32[]{:S(2)}) collective-permute-start(bf16[1,2,128,2048]{3,2,1,0:T(8,128)(2,1)} %all-gather.2.cloned.1.call-done), channel_id=1, source_target_pairs={{4,0},{8,4},{12,8},{16,12},{20,16},{24,20},{28,24},{5,1},{9,5},{13... | collective-permute-start | bytes 3145736 | tf_op jit(solution)/shard_map/ppermute | solution.py:19
  34.2 48.0 %collective-permute-start = (bf16[1,2,128,2048]{3,2,1,0:T(8,128)(2,1)}, bf16[1,2,128,2048]{3,2,1,0:T(8,128)(2,1)}, u32[]{:S(2)}, u32[]{:S(2)}) collective-permute-start(bf16[1,2,128,2048]{3,2,1,0:T(8,128)(2,1)} %all-gather.2.cloned.1.call-done), channel_id=1, source_target_pairs={{0,4},{4,8},{8,12},{12,16},{16,20},{20,24},{24,28},{1,5},{5,9},{9,... | collective-permute-start | bytes 3145736 | tf_op jit(solution)/shard_map/ppermute | solution.py:17
  42.5 39.7 %copy-start = (bf16[1,2,128,2048]{3,2,1,0:T(8,128)(2,1)S(1)}, bf16[1,2,128,2048]{3,2,1,0:T(8,128)(2,1)}, u32[]{:S(2)}) copy-start(bf16[1,2,128,2048]{3,2,1,0:T(8,128)(2,1)} %all-gather.2.cloned.1.call-done) | copy-start | bytes 3145732
  59.7 27.2 %copy-start.2 = (bf16[1,2,128,2048]{3,2,1,0:T(8,128)(2,1)}, bf16[1,2,128,2048]{3,2,1,0:T(8,128)(2,1)S(1)}, u32[]{:S(2)}) copy-start(bf16[1,2,128,2048]{3,2,1,0:T(8,128)(2,1)S(1)} %collective-permute-done.1) | copy-start | bytes 3145732
  99.9 2.8 %copy-start.1 = (bf16[1,2,128,2048]{3,2,1,0:T(8,128)(2,1)S(1)}, bf16[1,2,128,2048]{3,2,1,0:T(8,128)(2,1)}, u32[]{:S(2)}) copy-start(bf16[1,2,128,2048]{3,2,1,0:T(8,128)(2,1)} %all-gather.2.cloned.1.call-done) | copy-start | bytes 3145732
  99.9 2.8 %copy-start.3 = (bf16[1,2,128,2048]{3,2,1,0:T(8,128)(2,1)S(1)}, bf16[1,2,128,2048]{3,2,1,0:T(8,128)(2,1)}, u32[]{:S(2)}) copy-start(bf16[1,2,128,2048]{3,2,1,0:T(8,128)(2,1)} %copy-done.2) | copy-start | bytes 3145732
Sparse Core Ops, SparseCore 0:
  8.9 23.9 all-gather.1
  105.8 19.5 all-reduce.1
where the time goes:
time: 160 us
  waiting for transfers between devices  79.5 us (50%)
  other arithmetic  27.6 us (17%)
  between operations  14.3 us (9%)
  blocking collectives  11.2 us (7%)
  starting transfers between devices  11.1 us (7%)
  matrix products  8.34 us (5%)
  local copies, waits for them, and re-layouts  7.44 us (5%)
    ppermute x1, waiting for transfers between devices, with_halo(): lax.ppermute(tail, axis, [(i, (i + 1) % count) for i in range(ends)])  22.5 us
    all_gather x1, waiting for transfers between devices, on_device(): full_time = lax.all_gather(subject_data, 'tm', axis=3, tiled=True)  21.4 us
    psum x1, waiting for transfers between devices, subject_mean(): total = lax.psum(moved, 'subj')  19.7 us
    ppermute x1, waiting for transfers between devices, with_halo(): lax.ppermute(head, axis, [((i + 1) % count, i) for i in range(ends)])  15.2 us
    unnamed x1, other arithmetic  11.7 us
    all_to_all x1, blocking collectives, on_device(): lax.all_to_all(averaged, 'tm', split_axis=2, concat_axis=0, tiled=True)  11.2 us
    ppermute x1, starting transfers between devices, with_halo(): lax.ppermute(tail, axis, [(i, (i + 1) % count) for i in range(ends)])  5.54 us
    all_to_all x1, starting transfers between devices, on_device(): lax.all_to_all(template, 'tm', split_axis=0, concat_axis=2, tiled=True)  4.25 us
  transfers between devices with their start and end apart: 5, of which 4 were waited for; matrix products, arithmetic and copies ran while one was open for 3% of the time, Pallas kernels for 0%

commit v1 on v0

--- a/solution.py
+++ b/solution.py
@@ -4,6 +4,21 @@
 from jax.sharding import PartitionSpec as P
 
 ITERS = 3
+
+
+def clear_the_roots(inp):
+    high = lax.axis_size("tm")
+    block_out = lax.axis_index("tm")
+    v_next, z1 = (high, block_out)
+    current_block, left_arr = (inp, 1)
+    while left_arr < v_next:
+        all_rows = tuple(((tick, tick ^ left_arr) for tick in range(v_next)))
+        before = lax.ppermute(current_block, "tm", all_rows)
+        w2 = jnp.concatenate([current_block, before], axis=3)
+        tile_out = jnp.concatenate([before, current_block], axis=3)
+        current_block = jnp.where(z1 & left_arr == 0, w2, tile_out)
+        left_arr = 2 * left_arr
+    return current_block
 
 
 def with_halo(cells, sides, width):
@@ -74,7 +89,7 @@
     first = lax.axis_index("tm") * share
     my_offsets = lax.dynamic_slice_in_dim(offsets, first, share, 0)
     my_mask = lax.dynamic_slice_in_dim(mask_all, first, share, 0)
-    full_time = lax.all_gather(subject_data, "tm", axis=3, tiled=True)
+    full_time = clear_the_roots(subject_data)
     extended = with_halo(full_time, (("slab", 1),), blocks_here)
     mine = lax.all_to_all(template, "tm", split_axis=0, concat_axis=2, tiled=True)
     col_norm = lax.rsqrt(square_sum(extended) + 1e-06)

time: 160 us -> 152 us (0.950)
  waiting for transfers between devices: 79.5 us -> 67.8 us
  starting transfers between devices: 11.1 us -> 13.4 us
    all_gather x1 -> x0, waiting for transfers between devices: 21.4 us -> none  [on_device(): full_time = lax.all_gather(subject_data, 'tm', axis=3, tiled=True)]
    ppermute x0 -> x1, waiting for transfers between devices: none -> 9.43 us  [clear_the_roots(): before = lax.ppermute(current_block, 'tm', all_rows)]
    ppermute x0 -> x1, starting transfers between devices: none -> 2.97 us  [clear_the_roots(): before = lax.ppermute(current_block, 'tm', all_rows)]
    select_n x0 -> x1, other arithmetic: none -> 1.69 us  [clear_the_roots(): current_block = jnp.where(z1 & left_arr == 0, w2, tile_out)]
where the time goes in v1:
time: 152 us
  waiting for transfers between devices  67.8 us (45%)
  other arithmetic  28.9 us (19%)
  between operations  14.3 us (9%)
  starting transfers between devices  13.4 us (9%)
  blocking collectives  11.2 us (7%)
  local copies, waits for them, and re-layouts  8.1 us (5%)
  matrix products  7.86 us (5%)
    ppermute x1, waiting for transfers between devices, with_halo(): lax.ppermute(tail, axis, [(i, (i + 1) % count) for i in range(ends)])  22.4 us
    psum x1, waiting for transfers between devices, subject_mean(): total = lax.psum(moved, 'subj')  20.9 us
    ppermute x1, waiting for transfers between devices, with_halo(): lax.ppermute(head, axis, [((i + 1) % count, i) for i in range(ends)])  15.1 us
    unnamed x1, other arithmetic  11.7 us
    all_to_all x1, blocking collectives, on_device(): lax.all_to_all(averaged, 'tm', split_axis=2, concat_axis=0, tiled=True)  11.2 us
    ppermute x1, waiting for transfers between devices, clear_the_roots(): before = lax.ppermute(current_block, 'tm', all_rows)  9.43 us
    ppermute x1, starting transfers between devices, with_halo(): lax.ppermute(tail, axis, [(i, (i + 1) % count) for i in range(ends)])  5.58 us
    reduce_sum x3, other arithmetic, balance(): jnp.sum(kernel * row_weight, axis=1, keepdims=True) + filler  4.12 us
  transfers between devices with their start and end apart: 5, of which 4 were waited for; matrix products, arithmetic and copies ran while one was open for 3% of the time, Pallas kernels for 0%

profile of v1, /device:TPU:0, one launch (start us, length us, event | category | flops | bytes accessed | tf_op | source)
XLA Modules:
  0.0 151.6 jit_solution(15554880157844449094)
XLA Ops:
  6.5 3.0 %collective-permute-start = (bf16[1,2,128,1024]{3,2,1,0:T(8,128)(2,1)}, bf16[1,2,128,1024]{3,2,1,0:T(8,128)(2,1)S(1)}, u32[]{:S(2)}, u32[]{:S(2)}) collective-permute-start(bf16[1,2,128,1024]{3,2,1,0:T(8,128)(2,1)} %param.4), channel_id=1, source_target_pairs={{0,1},{1,0},{2,3},{3,2},{4,5},{5,4},{6,7},{7,6},{8,9},{9,8},{10,11... | collective-permute-start | bytes 1572872 | tf_op jit(solution)/shard_map/ppermute | solution.py:16
  9.5 3.5 %all-to-all-start = ((bf16[2,128,1024]{2,1,0:T(8,128)(2,1)}), bf16[2,128,1024]{2,1,0:T(8,128)(2,1)S(1)}, u32[]{:S(2)}, u32[]{:S(2)}) async-start(bf16[2,128,1024]{2,1,0:T(8,128)(2,1)} %param.5), calls=%async_computation | async-start | bytes 1048576 | tf_op jit(solution)/shard_map/all_to_all | solution.py:94
  13.1 9.4 %collective-permute-done = bf16[1,2,128,1024]{3,2,1,0:T(8,128)(2,1)S(1)} collective-permute-done((bf16[1,2,128,1024]{3,2,1,0:T(8,128)(2,1)}, bf16[1,2,128,1024]{3,2,1,0:T(8,128)(2,1)S(1)}, u32[]{:S(2)}, u32[]{:S(2)}) %collective-permute-start) | collective-permute-done | bytes 524320 | tf_op jit(solution)/shard_map/ppermute | solution.py:16
  22.5 1.7 %maximum_select_fusion = bf16[1,2,128,2048]{3,2,1,0:T(8,128)(2,1)S(1)} fusion(bf16[1,2,128,1024]{3,2,1,0:T(8,128)(2,1)S(1)} %collective-permute-done, bf16[1,2,128,1024]{3,2,1,0:T(8,128)(2,1)} %param.4, pred[]{:T(512)S(6)} %eq.29), kind=kLoop, calls=%fused_computation.32 | loop fusion | flops 4718592 | bytes 2097153 | tf_op jit(solution)/shard_map/jit(_where)/select_n | solution.py:19
  24.2 1.3 collective-permute-start.2
  25.5 5.6 %collective-permute-start.1 = (bf16[1,2,128,2048]{3,2,1,0:T(8,128)(2,1)S(1)}, bf16[1,2,128,2048]{3,2,1,0:T(8,128)(2,1)}, u32[]{:S(2)}, u32[]{:S(2)}) collective-permute-start(bf16[1,2,128,2048]{3,2,1,0:T(8,128)(2,1)S(1)} %maximum_select_fusion), channel_id=1, source_target_pairs={{0,4},{4,8},{8,12},{12,16},{16,20},{20,24},{24,28},{1,5},{5,9},{9,... | collective-permute-start | bytes 3145736 | tf_op jit(solution)/shard_map/ppermute | solution.py:32
  31.1 0.6 fusion.25
  32.4 0.5 copy.16
  33.0 1.2 reshape.379
  34.5 15.1 %collective-permute-done.2 = bf16[1,2,128,2048]{3,2,1,0:T(8,128)(2,1)S(1)} collective-permute-done((bf16[1,2,128,2048]{3,2,1,0:T(8,128)(2,1)S(1)}, bf16[1,2,128,2048]{3,2,1,0:T(8,128)(2,1)S(1)}, u32[]{:S(2)}, u32[]{:S(2)}) %collective-permute-start.2) | collective-permute-done | bytes 1048608 | tf_op jit(solution)/shard_map/ppermute | solution.py:34
  49.6 22.4 %collective-permute-done.1 = bf16[1,2,128,2048]{3,2,1,0:T(8,128)(2,1)} collective-permute-done((bf16[1,2,128,2048]{3,2,1,0:T(8,128)(2,1)S(1)}, bf16[1,2,128,2048]{3,2,1,0:T(8,128)(2,1)}, u32[]{:S(2)}, u32[]{:S(2)}) %collective-permute-start.1) | collective-permute-done | bytes 1048608 | tf_op jit(solution)/shard_map/ppermute | solution.py:32
  71.9 1.8 %fusion = f32[6,128]{1,0:T(8,128)S(1)} fusion(bf16[1,2,128,2048]{3,2,1,0:T(8,128)(2,1)S(1)} %collective-permute-done.2, bf16[1,2,128,2048]{3,2,1,0:T(8,128)(2,1)S(1)} %maximum_select_fusion, bf16[1,2,128,2048]{3,2,1,0:T(8,128)(2,1)} %collective-permute-done.1), kind=kLoop, calls=%fused_computation.3 | loop fusion | flops 7863552 | bytes 3148800 | tf_op jit(solution)/shard_map/...t,...t->.../dot_general | solution.py:57
  73.8 0.6 gather_fusion.1
  74.3 2.7 %convolution_bitcast_fusion.3 = f32[128,6,128]{0,2,1:T(8,128)S(1)} fusion(bf16[128,2048,1]{1,0,2:T(8,128)(2,1)} %reshape.379, bf16[1,2,128,2048]{3,2,1,0:T(8,128)(2,1)} %copy-done, bf16[1,2,128,2048]{3,2,1,0:T(8,128)(2,1)S(1)} %maximum_select_fusion, bf16[1,2,128,2048]{3,2,1,0:T(8,128)(2,1)} %collective-permute-done.1), kind=kOutput, calls=%fused_computation.31 | convolution fusion | flops 405798912 | bytes 4063232 | tf_op jit(solution)/shard_map/while/body/eval_jaxpr/it,sejt->siej/dot_general | solution.py:61
  77.0 0.7 gather_fusion
  77.7 0.8 fusion.27
  78.6 1.4 multiply_reduce_fusion.5
  80.0 1.3 multiply_reduce_fusion.4
  81.4 1.4 multiply_reduce_fusion.3
  82.8 1.3 multiply_reduce_fusion.2
  84.2 1.4 multiply_reduce_fusion.1
  85.6 1.3 multiply_reduce_fusion
  87.0 2.3 %fusion.15 = bf16[128,27,128]{0,2,1:T(8,128)(2,1)} fusion(f32[27,128,128]{1,2,0:T(8,128)S(1)} %gather_fusion, f32[128]{0:T(128)S(1)} %multiply_reduce_fusion, f32[27,128]{1,0:T(8,128)S(1)} %add_divide_fusion, f32[27]{0:T(128)S(1)} %get-tuple-element.20, f32[27,128]{1,0:T(8,128)S(1)} %broadcast_select_fusion, f32[128]{0:T(128)S(1)} %add_rsqrt_fusion.1, ...), kind=kLoop, calls=%fused_computation.29 | loop fusion | flops 3538944 | bytes 2683015 | tf_op jit(solution)/shard_map/while/body/eval_jaxpr/convert_element_type | solution.py:53
  89.3 2.0 %copy.17 = bf16[128,27,128]{2,1,0:T(8,128)(2,1)S(1)} copy(bf16[128,27,128]{0,2,1:T(8,128)(2,1)} %fusion.15) | data formatting | bytes 1769472 | tf_op jit(solution)/shard_map/while/body/eval_jaxpr/convert_element_type | solution.py:53
  91.6 2.0 %convolution_bitcast_fusion = f32[128,2048]{1,0:T(8,128)S(1)} fusion(bf16[128,6,128]{2,1,0:T(8,128)(2,1)S(1)} %get-tuple-element.32, bf16[1,2,128,2048]{3,2,1,0:T(8,128)(2,1)S(1)} %copy-done.1, bf16[1,2,128,2048]{3,2,1,0:T(8,128)(2,1)S(1)} %maximum_select_fusion, bf16[1,2,128,2048]{3,2,1,0:T(8,128)(2,1)} %collective-permute-done.1), kind=kOutput, calls=%fused_computation.5 | convolution fusion | flops 405798912 | bytes 4390912 | tf_op jit(solution)/shard_map/while/body/eval_jaxpr/siej,sejt->it/dot_general | solution.py:75
  93.6 3.0 %fusion.2 = f32[1,128,2048]{2,1,0:T(8,128)} fusion(f32[128,2048]{1,0:T(8,128)S(1)} %convolution_bitcast_fusion, bf16[128,6,128]{2,1,0:T(8,128)(2,1)S(1)} %get-tuple-element.23, bf16[1,2,128,2048]{3,2,1,0:T(8,128)(2,1)S(1)} %copy-done.1, bf16[1,2,128,2048]{3,2,1,0:T(8,128)(2,1)S(1)} %maximum_select_fusion, bf16[1,2,128,2048]{3,2,1,0:T(8,128)(2,1)} %collective-permute-done.1), kind=kOutput, calls=%fused_computation.8 | convolution fusion | flops 406061056 | bytes 5439488 | tf_op jit(solution)/shard_map/while/body/eval_jaxpr/siej,sejt->it/dot_general | solution.py:74
  96.6 20.9 %all-reduce.2.cloned.1.call-done = f32[1,128,2048]{2,1,0:T(8,128)} async-done(((f32[1,128,2048]{2,1,0:T(8,128)}), f32[1,128,2048]{2,1,0:T(8,128)}) %all-reduce.2.cloned.1.call-update) | async-done | bytes 1048592 | tf_op jit(solution)/shard_map/psum | solution.py:79
  117.5 1.3 multiply_convert_fusion
  118.8 0.8 copy.20
  120.1 11.7 %reduce.12 = bf16[2048,128]{1,0:T(8,128)(2,1)S(1)} reduce(bf16[2048,1,128]{2,1,0:T(2,128)(2,1)S(1)} %bitcast.110, bf16[]{:T(256)} %broadcast.458), dimensions={1}, to_apply=%bitcast.98.reduce_sub_computation | reduce | bytes 1048578
  132.0 11.2 %all_to_all.33 = bf16[2,2,65536]{2,1,0:T(2,128)(2,1)S(1)} all-to-all(bf16[2,2,65536]{2,1,0:T(2,128)(2,1)S(1)} %reshape.387), channel_id=1, replica_groups=mesh['slab'=8,'subj'=2,'tm'=2] {'tm'}, dimensions={0} | all-to-all | bytes 1048576 | tf_op jit(solution)/shard_map/all_to_all | solution.py:106
  143.8 1.0 copy.21
  (34 shorter events, 2.3 us)
Async XLA Ops:
  6.5 24.5 %copy-start.2 = (s32[2,27]{1,0:T(2,128)S(1)}, s32[2,27]{1,0:T(2,128)}, u32[]{:S(2)}) copy-start(s32[2,27]{1,0:T(2,128)} %param.6) | copy-start | bytes 652
  6.5 24.5 %copy-start.3 = (s32[2,27]{1,0:T(2,128)S(1)}, s32[2,27]{1,0:T(2,128)}, u32[]{:S(2)}) copy-start(s32[2,27]{1,0:T(2,128)} %param.7) | copy-start | bytes 652
  6.5 15.9 %collective-permute-start = (bf16[1,2,128,1024]{3,2,1,0:T(8,128)(2,1)}, bf16[1,2,128,1024]{3,2,1,0:T(8,128)(2,1)S(1)}, u32[]{:S(2)}, u32[]{:S(2)}) collective-permute-start(bf16[1,2,128,1024]{3,2,1,0:T(8,128)(2,1)} %param.4), channel_id=1, source_target_pairs={{0,1},{1,0},{2,3},{3,2},{4,5},{5,4},{6,7},{7,6},{8,9},{9,8},{10,11... | collective-permute-start | bytes 1572872 | tf_op jit(solution)/shard_map/ppermute | solution.py:16
  9.5 22.9 %all-to-all-start = ((bf16[2,128,1024]{2,1,0:T(8,128)(2,1)}), bf16[2,128,1024]{2,1,0:T(8,128)(2,1)S(1)}, u32[]{:S(2)}, u32[]{:S(2)}) async-start(bf16[2,128,1024]{2,1,0:T(8,128)(2,1)} %param.5), calls=%async_computation | async-start | bytes 1048576 | tf_op jit(solution)/shard_map/all_to_all | solution.py:94
  13.0 104.5 %all-reduce.2.cloned.1.call-start = ((), (), s32[]{:S(2)}) async-start(), calls=%async_computation.2 | async-start | bytes 2097152 | tf_op jit(solution)/shard_map/psum | solution.py:79
  24.2 25.4 %collective-permute-start.2 = (bf16[1,2,128,2048]{3,2,1,0:T(8,128)(2,1)S(1)}, bf16[1,2,128,2048]{3,2,1,0:T(8,128)(2,1)S(1)}, u32[]{:S(2)}, u32[]{:S(2)}) collective-permute-start(bf16[1,2,128,2048]{3,2,1,0:T(8,128)(2,1)S(1)} %maximum_select_fusion), channel_id=1, source_target_pairs={{4,0},{8,4},{12,8},{16,12},{20,16},{24,20},{28,24},{5,1},{9,5},{13... | collective-permute-start | bytes 3145736 | tf_op jit(solution)/shard_map/ppermute | solution.py:34
  25.5 46.4 %collective-permute-start.1 = (bf16[1,2,128,2048]{3,2,1,0:T(8,128)(2,1)S(1)}, bf16[1,2,128,2048]{3,2,1,0:T(8,128)(2,1)}, u32[]{:S(2)}, u32[]{:S(2)}) collective-permute-start(bf16[1,2,128,2048]{3,2,1,0:T(8,128)(2,1)S(1)} %maximum_select_fusion), channel_id=1, source_target_pairs={{0,4},{4,8},{8,12},{12,16},{16,20},{20,24},{24,28},{1,5},{5,9},{9,... | collective-permute-start | bytes 3145736 | tf_op jit(solution)/shard_map/ppermute | solution.py:32
  49.5 24.2 %copy-start = (bf16[1,2,128,2048]{3,2,1,0:T(8,128)(2,1)}, bf16[1,2,128,2048]{3,2,1,0:T(8,128)(2,1)S(1)}, u32[]{:S(2)}) copy-start(bf16[1,2,128,2048]{3,2,1,0:T(8,128)(2,1)S(1)} %collective-permute-done.2) | copy-start | bytes 3145732
  89.3 2.3 %copy-start.1 = (bf16[1,2,128,2048]{3,2,1,0:T(8,128)(2,1)S(1)}, bf16[1,2,128,2048]{3,2,1,0:T(8,128)(2,1)}, u32[]{:S(2)}) copy-start(bf16[1,2,128,2048]{3,2,1,0:T(8,128)(2,1)} %copy-done) | copy-start | bytes 3145732
Sparse Core Ops, SparseCore 0:
  96.7 20.7 all-reduce.1
